TPU v7x, 32 devices: a whole 2x2x4 slice. The times are simulated.
32 devices in a mesh: segment: 4 (over z), ctx: 2 (over x), dp: 4 (over y, core).
Axes of the slice: x: 2, y: 2, z: 4, core: 2. Of those that a mesh axis runs over, the one named last changes fastest.
Arguments:
- qkv: bfloat16 [4, 4, 320, 3, 2560], P('segment', 'dp', 'ctx'), may hold values from -24 to 24
- qk_gain: float32 [4, 2, 2560], P('segment'), may hold values from 1.5 to 2.5
- mod_weight: float32 [4, 256, 2560], P('segment'), may hold values from -0.375 to 0.375
- positions: int32 [4, 320], P('dp', 'ctx'), may hold values from 0 to 75599
- timesteps: int32 [4, 4], P('segment', 'dp'), may hold values from 0 to 999
- cotangent: bfloat16 [4, 4, 320, 2560], P('segment', 'dp', 'ctx'), may hold values from -6 to 6
Outputs:
- attn_out: bfloat16 [4, 4, 320, 2560], P('segment', 'dp', 'ctx')
- gate_grad: float32 [4, 256, 2560], P('segment', ('ctx', 'dp'))
All inputs are finite; a program needn't handle non-finite values.
Results may differ from a plain program's by a relative error of at most 0.012.
Values may be sent and summed in bfloat16 or wider, within the bound.
A program may use at most 128 MiB of HBM per device.

v0:
```python
import jax
import jax.numpy as jnp
from jax import lax
from jax.sharding import PartitionSpec as P

HEADS = 20
HEAD_DIM = 128
FREQS = 256
GRID_ROWS = 45
GRID_COLS = 80


def shifted(value, axis, by):
    length = lax.axis_size(axis)
    return lax.ppermute(value, axis, [(i, (i + by) % length) for i in range(length)])


def rope_tables(pos):
    half = HEAD_DIM // 2
    side = HEAD_DIM // 6
    first = half - 2 * side
    frame = (pos // (GRID_ROWS * GRID_COLS)).astype(jnp.float32)
    row = (pos // GRID_COLS % GRID_ROWS).astype(jnp.float32)
    col = (pos % GRID_COLS).astype(jnp.float32)
    pair = jnp.arange(half, dtype=jnp.int32)
    group = jnp.where(pair < first, 0, jnp.where(pair < first + side, 1, 2))
    offset = jnp.where(group == 0, 0, jnp.where(group == 1, first, first + side))
    pairs_in = jnp.where(group == 0, first, side).astype(jnp.float32)
    freq = 10000.0 ** (-(pair - offset).astype(jnp.float32) / pairs_in)
    coord = jnp.where(
        group[None, :] == 0,
        frame[:, None],
        jnp.where(group[None, :] == 1, row[:, None], col[:, None]),
    )
    angle = coord * freq[None, :]
    cosine = jnp.tile(jnp.concatenate([jnp.cos(angle), jnp.cos(angle)], axis=1), (1, HEADS))
    sine = jnp.tile(jnp.concatenate([jnp.sin(angle), jnp.sin(angle)], axis=1), (1, HEADS))
    return (cosine, sine)


def rotate(values, cosine, sine):
    count = values.shape[0]
    half = HEAD_DIM // 2
    shaped = values.reshape(count, HEADS, HEAD_DIM)
    turned = jnp.concatenate([-shaped[:, :, half:], shaped[:, :, :half]], axis=2).reshape(
        count, HEADS * HEAD_DIM
    )
    return values * cosine + turned * sine


def normalize(values, gain):
    mean_sq = jnp.mean(values * values, axis=-1, keepdims=True)
    return values * lax.rsqrt(mean_sq + 1e-06) * gain


def embed(step):
    count = FREQS // 2
    freq = 10000.0 ** (-jnp.arange(count, dtype=jnp.float32) / count)
    angle = step.astype(jnp.float32) * freq
    return jnp.concatenate([jnp.cos(angle), jnp.sin(angle)])


def head_major(rows):
    count = rows.shape[0]
    return rows.reshape(count, HEADS, HEAD_DIM).transpose(1, 0, 2)


def section_attention(block, gains, pos):
    count = block.shape[0]
    width = HEADS * HEAD_DIM
    cosine, sine = rope_tables(pos)
    queries = rotate(normalize(block[:, 0].astype(jnp.float32), gains[0]), cosine, sine).astype(
        jnp.bfloat16
    )
    keys = rotate(normalize(block[:, 1].astype(jnp.float32), gains[1]), cosine, sine).astype(
        jnp.bfloat16
    )
    queries = head_major(queries)
    keys = head_major(keys)
    values = head_major(block[:, 2])
    scale = 1.0 / HEAD_DIM**0.5

    def attend(carry, key_block, value_block):
        peak, total, accum = carry
        scores = (
            jnp.einsum("hqd,hkd->hqk", queries, key_block, preferred_element_type=jnp.float32)
            * scale
        )
        new_peak = jnp.maximum(peak, jnp.max(scores, axis=2))
        fade = jnp.exp(peak - new_peak)
        expo = jnp.exp(scores - new_peak[:, :, None])
        total = total * fade + jnp.sum(expo, axis=2)
        update = jnp.einsum(
            "hqk,hkd->hqd",
            expo.astype(jnp.bfloat16),
            value_block,
            preferred_element_type=jnp.float32,
        )
        return (new_peak, total, accum * fade[:, :, None] + update)

    def fold_keys(carry, piece):
        key_heads, value_heads = piece
        length = key_heads.shape[1]
        if length > 512 and length % 512 == 0:

            def step_block(index, state):
                begin = (index * 512).astype(jnp.int32)
                key_part = lax.dynamic_slice_in_dim(key_heads, begin, 512, 1)
                value_part = lax.dynamic_slice_in_dim(value_heads, begin, 512, 1)
                return attend(state, key_part, value_part)

            return lax.fori_loop(0, length // 512, step_block, carry)
        return attend(carry, key_heads, value_heads)

    start_state = (
        jnp.full((HEADS, count), -1e30, jnp.float32),
        jnp.zeros((HEADS, count), jnp.float32),
        jnp.zeros((HEADS, count, HEAD_DIM), jnp.float32),
    )
    peak, total, accum = fold_keys(
        start_state,
        (
            lax.all_gather(keys, "ctx", axis=1, tiled=True),
            lax.all_gather(values, "ctx", axis=1, tiled=True),
        ),
    )
    return (accum / total[:, :, None]).transpose(1, 0, 2).reshape(count, width)


def local(qkv, qk_gain, mod_weight, positions, timesteps, cotangent):
    later_gains = shifted(qk_gain, "segment", -1)
    local_attn = section_attention(qkv[0, 0], later_gains[0], positions[0])
    attn = shifted(local_attn.astype(jnp.bfloat16), "segment", 1).astype(local_attn.dtype)
    emb = embed(timesteps[0, 0])
    gate = jnp.dot(emb, mod_weight[0], precision=lax.Precision.HIGHEST)
    attn_out = (attn * gate).astype(jnp.bfloat16)[None, None]
    chan = jnp.sum(attn * cotangent[0, 0].astype(jnp.float32), axis=0)
    term = emb[:, None] * chan[None, :]
    gate_grad = lax.psum_scatter(term, ("ctx", "dp"), scatter_dimension=0, tiled=True)
    return (attn_out, gate_grad[None])


def solution(mesh):
    return jax.shard_map(
        local,
        mesh=mesh,
        in_specs=(
            P("segment", "dp", "ctx", None, None),
            P("segment", None, None),
            P("segment", None, None),
            P("dp", "ctx"),
            P("segment", "dp"),
            P("segment", "dp", "ctx", None),
        ),
        out_specs=(P("segment", "dp", "ctx", None), P("segment", ("ctx", "dp"), None)),
        check_vma=False,
    )
```

profile of v0, /device:TPU:0, one launch (start us, length us, event | category | flops | bytes accessed | tf_op | source)
XLA Modules:
  0.0 161.9 jit_solution(11266359706596007274)
XLA Ops:
  7.2 0.0 copy-start
  7.2 0.0 all-gather.3.cloned.1.call-start
  7.2 5.1 %collective-permute-start = (f32[1,2,2560]{2,1,0:T(2,128)}, f32[1,2,2560]{2,1,0:T(2,128)S(1)}, u32[]{:S(2)}, u32[]{:S(2)}) collective-permute-start(f32[1,2,2560]{2,1,0:T(2,128)} %param.7), channel_id=1, source_target_pairs={{0,24},{8,0},{16,8},{24,16},{1,25},{9,1},{17,9},{25,17},{2,26},{10... | collective-permute-start | bytes 61448 | tf_op jit(solution)/shard_map/ppermute | solution.py:15
  12.4 0.7 broadcast_divide_fusion.1
  13.0 0.7 compare_reduce_fusion
  13.8 0.0 copy-start.4
  13.8 3.7 %slice_convert_fusion.1 = (f32[160,1,2560]{2,0,1:T(8,128)}, bf16[160,1,2560]{2,0,1:T(8,128)(2,1)S(1)}, f32[160,1,2560]{2,0,1:T(8,128)}) fusion(bf16[160,3,2560]{2,0,1:T(8,128)(2,1)} %bitcast.57), kind=kLoop, calls=%fused_computation.39 | loop fusion | flops 819200 | bytes 6553600 | tf_op jit(solution)/shard_map/convert_element_type | solution.py:72
  17.5 0.0 copy-done.4
  17.5 0.8 multiply_reduce_fusion.2
  18.4 0.6 add_rsqrt_fusion
  19.0 0.4 fusion.34
  19.4 0.7 pad_maximum_fusion
  20.1 2.6 %reshape.203 = f32[160,20,128]{2,1,0:T(8,128)} reshape(f32[160,1,2560]{2,0,1:T(8,128)} %get-tuple-element.10) | data formatting | bytes 3276800 | tf_op jit(solution)/shard_map/convert_element_type | solution.py:75
  22.7 0.0 collective-permute-done
  22.7 0.1 slice_reduce_fusion.1
  22.8 2.0 %fusion.16 = f32[160,20,128]{2,0,1:T(8,128)S(1)} fusion(f32[160,20,128]{2,1,0:T(8,128)} %reshape.203, f32[20,128]{1,0:T(8,128)S(1)} %bitcast.61, f32[160]{0:T(256)} %add_rsqrt_fusion), kind=kLoop, calls=%fused_computation.25 | loop fusion | flops 819200 | bytes 3287680 | tf_op jit(solution)/shard_map/mul | solution.py:53
  24.8 0.0 copy-start.3
  24.8 0.0 copy-start.6
  24.8 0.0 copy-start.8
  24.8 0.6 slice_negate_fusion
  25.4 0.9 copy-done.3
  26.3 0.0 copy-done.6
  26.3 0.0 copy-done.8
  26.3 1.6 fusion.26
  27.9 0.0 all-gather.3.cloned.1.call-update
  27.9 0.0 all-gather.5.cloned.1.call-start
  28.0 1.5 reshape_squeeze.3
  29.5 2.2 %copy.24 = bf16[160,20,128]{2,0,1:T(8,128)(2,1)} copy(bf16[160,20,128]{2,1,0:T(8,128)(2,1)} %reshape_squeeze.3) | data formatting | bytes 1638400 | tf_op jit(solution)/shard_map/reshape;squeeze | solution.py:65
  31.7 0.0 all-gather.5.cloned.1.call-update
  31.7 0.0 reduce-scatter.2.cloned.1.call-start
  31.7 0.0 copy-start.9
  31.8 2.7 %reshape.202 = f32[160,20,128]{2,1,0:T(8,128)} reshape(f32[160,1,2560]{2,0,1:T(8,128)} %get-tuple-element.8) | data formatting | bytes 3276800 | tf_op jit(solution)/shard_map/convert_element_type | solution.py:72
  34.5 0.0 copy-done.9
  34.5 2.1 %fusion.17 = f32[160,20,128]{2,0,1:T(8,128)S(1)} fusion(f32[160,20,128]{2,1,0:T(8,128)} %reshape.202, f32[20,128]{1,0:T(8,128)S(1)} %bitcast.63, f32[160]{0:T(256)S(1)} %add_rsqrt_fusion.1), kind=kLoop, calls=%fused_computation.27 | loop fusion | flops 819200 | bytes 3287680 | tf_op jit(solution)/shard_map/mul | solution.py:53
  36.6 0.0 copy-start.1
  36.6 1.3 copy-done.1
  37.9 0.0 copy-start.7
  37.9 2.3 %slice_negate_fusion.1 = (f32[160,20,64]{2,0,1:T(8,128)}, f32[160,20,64]{2,0,1:T(8,128)}) fusion(f32[160,20,128]{2,0,1:T(8,128)S(1)} %fusion.17), kind=kLoop, calls=%fused_computation.14 | loop fusion | flops 204800 | bytes 3276800 | tf_op jit(solution)/shard_map/neg | solution.py:45
  40.2 14.1 %all-gather.3.cloned.1.call-done = bf16[20,320,128]{2,1,0:T(8,128)(2,1)} async-done(((bf16[20,160,128]{2,1,0:T(8,128)(2,1)}), bf16[20,320,128]{2,1,0:T(8,128)(2,1)}) %all-gather.3.cloned.1.call-update) | async-done | bytes 1638416 | tf_op jit(solution)/shard_map/all_gather | solution.py:123
  54.3 0.0 copy-done.7
  54.3 4.7 %multiply_reduce_fusion = (f32[20,160]{1,0:T(8,128)S(1)}, f32[20,160,320]{2,1,0:T(8,128)S(1)}) fusion(bf16[20,320,128]{2,1,0:T(8,128)(2,1)} %all-gather.3.cloned.1.call-done, f32[160,20,64]{2,0,1:T(8,128)} %get-tuple-element.12, f32[160,20,64]{2,0,1:T(8,128)} %get-tuple-element.11, f32[160,20,128]{2,0,1:T(8,128)} %copy-done.1, f32[160,128]{1,0:T(8,128)S(1)} %copy-done.7, ...), kind=kOutput, calls=%fused_computation.1 | convolution fusion | flops 266236800 | bytes 9187840 | tf_op jit(solution)/shard_map/hqd,hkd->hqk/dot_general | solution.py:86
  59.1 0.0 copy-start.2
  59.1 1.7 %fusion = f32[20,160]{1,0:T(8,128)S(1)} fusion(f32[20,160,320]{2,1,0:T(8,128)S(1)} %get-tuple-element.28, f32[20,160]{1,0:T(8,128)S(1)} %get-tuple-element.18), kind=kLoop, calls=%fused_computation.2 | loop fusion | flops 3068800 | bytes 4121600 | tf_op jit(solution)/shard_map/reduce_sum | solution.py:92
  60.8 0.5 copy-done.2
  61.3 23.1 %all-gather.5.cloned.1.call-done = bf16[20,320,128]{2,1,0:T(8,128)(2,1)} async-done(((bf16[20,160,128]{2,1,0:T(8,128)(2,1)}), bf16[20,320,128]{2,1,0:T(8,128)(2,1)}) %all-gather.5.cloned.1.call-update) | async-done | bytes 1638416 | tf_op jit(solution)/shard_map/all_gather | solution.py:124
  84.4 4.3 %fusion.20 = bf16[20,20,8,128]{3,2,1,0:T(8,128)(2,1)S(1)} fusion(bf16[20,320,128]{2,1,0:T(8,128)(2,1)} %all-gather.5.cloned.1.call-done, f32[20,160,320]{2,1,0:T(8,128)} %copy-done.2, f32[20,160]{1,0:T(8,128)S(1)} %get-tuple-element.18, f32[160,20]{0,1:T(8,128)S(1)} %bitcast_add_fusion.1, f32[160,20]{0,1:T(8,128)S(1)} %get-tuple-element.17), kind=kOutput, calls=%fused_computation.31 | convolution fusion | flops 266444800 | bytes 6592000 | tf_op jit(solution)/shard_map/hqk,hkd->hqd/dot_general | solution.py:93
  88.7 0.1 copy.23
  88.9 0.0 copy-start.5
  88.9 1.5 collective-permute-start.1
  91.1 0.1 fusion.40
  91.1 0.0 copy-done
  91.2 1.3 fusion.23
  92.5 18.1 %collective-permute-done.1 = bf16[160,2560]{1,0:T(8,128)(2,1)S(1)} collective-permute-done((bf16[160,2560]{1,0:T(8,128)(2,1)S(1)}, bf16[160,2560]{1,0:T(8,128)(2,1)S(1)}, u32[]{:S(2)}, u32[]{:S(2)}) %collective-permute-start.1) | collective-permute-done | bytes 819232 | tf_op jit(solution)/shard_map/ppermute | solution.py:15
  110.6 0.0 copy-done.5
  110.6 1.2 fusion.9
  111.8 1.7 %broadcast_multiply_fusion = f32[256,2560]{1,0:T(8,128)} fusion(f32[2560]{0:T(1024)S(1)} %get-tuple-element.15, f32[256]{0:T(256)S(1)} %pad_maximum_fusion.2), kind=kLoop, calls=%fused_computation.30 | loop fusion | flops 655360 | bytes 2632704 | tf_op jit(solution)/shard_map/mul | solution.py:138
  113.5 0.0 reduce-scatter.2.cloned.1.call-update
  113.5 41.9 %reduce-scatter.2.cloned.1.call-done = f32[32,2560]{1,0:T(8,128)} async-done(((f32[256,2560]{1,0:T(8,128)}), f32[32,2560]{1,0:T(8,128)}) %reduce-scatter.2.cloned.1.call-update) | async-done | bytes 327696 | tf_op jit(solution)/shard_map/reduce_scatter | solution.py:139
  (8 shorter events, 0.1 us)
Async XLA Ops:
  7.2 84.0 %copy-start = (f32[1,256,2560]{2,1,0:T(8,128)S(1)}, f32[1,256,2560]{2,1,0:T(8,128)}, u32[]{:S(2)}) copy-start(f32[1,256,2560]{2,1,0:T(8,128)} %param.8) | copy-start | bytes 7864324
  7.2 47.2 %all-gather.3.cloned.1.call-start = ((), (), s32[]{:S(2)}) async-start(), calls=%async_computation.1 | async-start | bytes 2457600 | tf_op jit(solution)/shard_map/all_gather | solution.py:123
  7.2 15.5 %collective-permute-start = (f32[1,2,2560]{2,1,0:T(2,128)}, f32[1,2,2560]{2,1,0:T(2,128)S(1)}, u32[]{:S(2)}, u32[]{:S(2)}) collective-permute-start(f32[1,2,2560]{2,1,0:T(2,128)} %param.7), channel_id=1, source_target_pairs={{0,24},{8,0},{16,8},{24,16},{1,25},{9,1},{17,9},{25,17},{2,26},{10... | collective-permute-start | bytes 61448 | tf_op jit(solution)/shard_map/ppermute | solution.py:15
  13.8 3.8 %copy-start.4 = (bf16[1,1,160,3,2560]{4,2,3,1,0:T(8,128)(2,1)S(1)}, bf16[1,1,160,3,2560]{4,2,3,1,0:T(8,128)(2,1)}, u32[]{:S(2)}) copy-start(bf16[1,1,160,3,2560]{4,2,3,1,0:T(8,128)(2,1)} %param.6) | copy-start | bytes 7372804
  24.8 1.5 copy-start.3
  24.8 1.5 copy-start.6
  24.8 1.5 copy-start.8
  27.9 56.5 %all-gather.5.cloned.1.call-start = ((), (), s32[]{:S(2)}) async-start(), calls=%async_computation.2 | async-start | bytes 2457600 | tf_op jit(solution)/shard_map/all_gather | solution.py:124
  31.7 123.7 %reduce-scatter.2.cloned.1.call-start = ((), (), s32[]{:S(2)}) async-start(), calls=%async_computation.3 | async-start | bytes 2949120 | tf_op jit(solution)/shard_map/reduce_scatter | solution.py:139
  31.7 2.7 %copy-start.9 = (f32[160]{0:T(256)S(1)}, f32[160]{0:T(256)}, u32[]{:S(2)}) copy-start(f32[160]{0:T(256)} %get-tuple-element.2) | copy-start | bytes 1924
  36.6 1.3 copy-start.1
  37.9 16.5 %copy-start.7 = (f32[160,128]{1,0:T(8,128)S(1)}, f32[160,128]{1,0:T(8,128)}, u32[]{:S(2)}) copy-start(f32[160,128]{1,0:T(8,128)} %get-tuple-element.30) | copy-start | bytes 245764
  59.1 2.2 %copy-start.2 = (f32[20,160,320]{2,1,0:T(8,128)}, f32[20,160,320]{2,1,0:T(8,128)S(1)}, u32[]{:S(2)}) copy-start(f32[20,160,320]{2,1,0:T(8,128)S(1)} %get-tuple-element.28) | copy-start | bytes 12288004
  88.9 21.7 %copy-start.5 = (bf16[1,1,160,2560]{3,2,1,0:T(8,128)(2,1)S(1)}, bf16[1,1,160,2560]{3,2,1,0:T(8,128)(2,1)}, u32[]{:S(2)}) copy-start(bf16[1,1,160,2560]{3,2,1,0:T(8,128)(2,1)} %param.11) | copy-start | bytes 2457604
  88.9 21.7 %collective-permute-start.1 = (bf16[160,2560]{1,0:T(8,128)(2,1)S(1)}, bf16[160,2560]{1,0:T(8,128)(2,1)S(1)}, u32[]{:S(2)}, u32[]{:S(2)}) collective-permute-start(bf16[160,2560]{1,0:T(8,128)(2,1)S(1)} %bitcast.60), channel_id=1, source_target_pairs={{0,8},{8,16},{16,24},{24,0},{1,9},{9,17},{17,25},{25,1},{2,10},{10... | collective-permute-start | bytes 2457608 | tf_op jit(solution)/shard_map/ppermute | solution.py:15
Sparse Core Ops, SparseCore 0:
  28.1 26.2 all-gather.2
  56.5 27.9 all-gather.4
  113.6 41.6 reduce-scatter.1
where the time goes:
time: 162 us
  waiting for transfers between devices  97.2 us (60%)
  other arithmetic  21 us (13%)
  between operations  14.6 us (9%)
  local copies, waits for them, and re-layouts  11.9 us (7%)
  matrix products  10.3 us (6%)
  starting transfers between devices  6.79 us (4%)
    reduce_scatter x1, waiting for transfers between devices, local(): lax.psum_scatter(term, ('ctx', 'dp'), scatter_dimension=0, tiled=True)  41.9 us
    all_gather x1, waiting for transfers between devices, section_attention(): lax.all_gather(values, 'ctx', axis=1, tiled=True)  23.1 us
    ppermute x2, waiting for transfers between devices, shifted(): lax.ppermute(value, axis, [(i, (i + by) % length) for i in range(length)])  18.1 us
    all_gather x1, waiting for transfers between devices, section_attention(): lax.all_gather(keys, 'ctx', axis=1, tiled=True)  14.1 us
    ppermute x2, starting transfers between devices, shifted(): lax.ppermute(value, axis, [(i, (i + by) % length) for i in range(length)])  6.67 us
    dot_general x1, matrix products, attend(): jnp.einsum('hqd,hkd->hqk', queries, key_block, preferred_element_type=jnp...  4.7 us
    dot_general x1, matrix products, attend(): jnp.einsum('hqk,hkd->hqd', expo.astype(jnp.bfloat16), value_block, prefer...  4.3 us
    mul x2, other arithmetic, normalize(): return values * lax.rsqrt(mean_sq + 1e-06) * gain  4.08 us
  transfers between devices with their start and end apart: 5, of which 4 were waited for; matrix products, arithmetic and copies ran while one was open for 18% of the time, Pallas kernels for 0%

commit v1 on v0

v1 whole, which is shorter than its diff:
```python
import functools
import math

import jax
import jax.numpy as jnp
import numpy as np
from jax import lax
from jax.experimental import pallas as pl
from jax.experimental.pallas import tpu as pltpu
from jax.sharding import PartitionSpec as P

HEAD_DIM = 128
GRID_ROWS = 45
GRID_COLS = 80
MESH = pl.DeviceIdType.MESH
LEAD = 8
LAG = 4


def sincos(angle):
    turns = jnp.floor(angle * (2.0 / math.pi) + 0.5)
    quad = turns.astype(jnp.int32)
    r = angle - turns * 1.5703125
    r = r - turns * 4.837512969970703125e-4
    r = r - turns * 7.549789948768648e-8
    z = r * r
    sine = r + r * z * (-1.6666654611e-1 + z * (8.3321608736e-3 - z * 1.9515295891e-4))
    cosine = 1.0 - 0.5 * z + z * z * (
        4.166664568298827e-2 + z * (-1.388731625493765e-3 + z * 2.443315711809948e-5)
    )
    swap = (quad & 1) == 1
    s = jnp.where(swap, cosine, sine)
    c = jnp.where(swap, sine, cosine)
    s = jnp.where((quad & 2) == 2, -s, s)
    c = jnp.where(((quad + 1) & 2) == 2, -c, c)
    return s, c


def rope_freqs():
    half = HEAD_DIM // 2
    side = HEAD_DIM // 6
    first = half - 2 * side
    rows = np.zeros((8, HEAD_DIM), np.float64)
    start = 0
    for group, count in enumerate((first, side, side)):
        for j in range(count):
            for lane in (start + j, start + j + half):
                rows[group, lane] = 10000.0 ** (-j / count)
        start += count
    return rows.astype(np.float32)


def body(
    S, C, D, heads, freqs,
    x_ref, gain_ref, w_ref, pos_ref, t_ref, cot_ref, freq_ref,
    out_ref, grad_ref,
    xv, wv, cotv, kv, qbuf, abuf, rbuf, gains, tbuf, ebuf, cbuf, gate, cosv, sinv,
    load_sem, kv_send, kv_recv, a_send, a_recv, g_send, g_recv, t_send, t_recv, c_send, c_recv,
):
    n = C * D
    count = x_ref.shape[1]
    rows = freqs // n
    hd = HEAD_DIM
    seg = lax.axis_index("segment")
    ctx = lax.axis_index("ctx")
    dp = lax.axis_index("dp")
    me = ctx * D + dp
    after = {"segment": lax.rem(seg + 1, S)}
    before = {"segment": lax.rem(seg + S - 1, S)}
    peers = []
    for r in range(1, n):
        p = lax.rem(me + r, n)
        peers.append({"ctx": p // D, "dp": lax.rem(p, D)})
    ring = [{"ctx": lax.rem(ctx + r, C)} for r in range(1, C)]

    def cols(h):
        return pl.ds(pl.multiple_of(h * hd, hd), hd)

    loads = [
        pltpu.make_async_copy(x_ref.at[1], xv.at[1], load_sem.at[1]),
        pltpu.make_async_copy(x_ref.at[0], xv.at[0], load_sem.at[0]),
        pltpu.make_async_copy(x_ref.at[2], xv.at[2], load_sem.at[2]),
        pltpu.make_async_copy(w_ref, wv, load_sem.at[3]),
        pltpu.make_async_copy(cot_ref, cotv, load_sem.at[4]),
    ]
    for load in loads:
        load.start()
    step = t_ref[0, 0].astype(jnp.float32)
    tbuf[0] = jnp.full((8, hd), step, jnp.float32)

    barrier = pltpu.get_barrier_semaphore()
    for who in peers + [after, before]:
        pl.semaphore_signal(barrier, inc=1, device_id=who, device_id_type=MESH)
    pl.semaphore_wait(barrier, n + 1)

    gain_copy = pltpu.make_async_remote_copy(
        src_ref=gain_ref, dst_ref=gains, send_sem=g_send, recv_sem=g_recv,
        device_id=before, device_id_type=MESH,
    )
    gain_copy.start()

    def send_values(h):
        for r in range(1, C):
            pltpu.make_async_remote_copy(
                src_ref=x_ref.at[2, :, cols(h)],
                dst_ref=kv.at[h, 1, pl.ds(r * count, count), :],
                send_sem=kv_send.at[h], recv_sem=kv_recv.at[h],
                device_id=ring[r - 1], device_id_type=MESH,
            ).start()

    def send_keys(h):
        for r in range(1, C):
            pltpu.make_async_remote_copy(
                src_ref=kv.at[h, 0, pl.ds(0, count), :],
                dst_ref=kv.at[h, 0, pl.ds(r * count, count), :],
                send_sem=kv_send.at[h], recv_sem=kv_recv.at[h],
                device_id=ring[r - 1], device_id_type=MESH,
            ).start()

    lead = min(LEAD, heads)

    @pl.loop(0, lead)
    def _(h):
        send_values(h)

    for r in range(1, n):
        pltpu.make_async_remote_copy(
            src_ref=tbuf.at[0], dst_ref=tbuf.at[r], send_sem=t_send, recv_sem=t_recv,
            device_id=peers[r - 1], device_id_type=MESH,
        ).start()

    pos = jnp.broadcast_to(pos_ref[...], (count, hd))
    frame = (pos // (GRID_ROWS * GRID_COLS)).astype(jnp.float32)
    row = (pos // GRID_COLS % GRID_ROWS).astype(jnp.float32)
    col = (pos % GRID_COLS).astype(jnp.float32)
    angle = frame * freq_ref[0:1, :] + row * freq_ref[1:2, :] + col * freq_ref[2:3, :]
    s, c = sincos(angle)
    lane = lax.broadcasted_iota(jnp.int32, (count, hd), 1)
    cosv[...] = c
    sinv[...] = jnp.where(lane < hd // 2, -s, s)

    def inverse_norm(which):
        def add(h, acc):
            x = xv[which, :, cols(h)].astype(jnp.float32)
            return acc + x * x

        total = lax.fori_loop(0, heads, add, jnp.zeros((count, hd), jnp.float32))
        mean = jnp.sum(total, axis=1, keepdims=True) / (heads * hd)
        return lax.rsqrt(mean + 1e-06)

    def turned(which, h, inv):
        x = xv[which, :, cols(h)].astype(jnp.float32)
        x = x * inv * gains[which : which + 1, cols(h)]
        return (x * cosv[...] + pltpu.roll(x, hd // 2, 1) * sinv[...]).astype(jnp.bfloat16)

    loads[0].wait()
    inv_k = inverse_norm(1)
    gain_copy.wait_recv()

    @pl.loop(0, heads)
    def _(h):
        kv[h, 0, 0:count, :] = turned(1, h, inv_k)
        send_keys(h)

        @pl.when(h + lead < heads)
        def _():
            send_values(h + lead)

    loads[1].wait()
    inv_q = inverse_norm(0)
    loads[2].wait()

    @pl.loop(0, heads)
    def _(h):
        qbuf[h] = turned(0, h, inv_q)
        kv[h, 1, 0:count, :] = xv[2, :, cols(h)]

    half = freqs // 2
    decay = -math.log(10000.0) / half
    index = lax.broadcasted_iota(jnp.int32, (half, hd), 0).astype(jnp.float32)
    es, ec = sincos(step * jnp.exp(index * decay))
    loads[3].wait()

    @pl.loop(0, heads)
    def _(h):
        part = wv[0:half, cols(h)] * ec + wv[half:freqs, cols(h)] * es
        gate[pl.ds(h, 1), :] = jnp.sum(part, axis=0, keepdims=True)

    if n > 1:
        pltpu.make_async_copy(tbuf.at[pl.ds(1, n - 1)], tbuf.at[pl.ds(1, n - 1)], t_recv).wait()
    at = lax.broadcasted_iota(jnp.int32, (rows, hd), 0) + me * rows
    freq = jnp.exp((at % half).astype(jnp.float32) * decay)
    for j in range(n):
        s, c = sincos(tbuf[j, 0:1, :] * freq)
        ebuf[j] = jnp.where(at < half, c, s)
    loads[4].wait()

    scale = 1.0 / hd**0.5

    def attend(h):
        arrived = kv.at[h, :, pl.ds(count, (C - 1) * count), :]
        pltpu.make_async_copy(arrived, arrived, kv_recv.at[h]).wait()
        scores = lax.dot_general(
            qbuf[h], kv[h, 0], (((1,), (1,)), ((), ())), preferred_element_type=jnp.float32
        ) * scale
        expo = jnp.exp(scores - jnp.max(scores, axis=1, keepdims=True))
        total = jnp.sum(expo, axis=1, keepdims=True)
        mixed = jnp.dot(expo.astype(jnp.bfloat16), kv[h, 1], preferred_element_type=jnp.float32)
        abuf[h] = (mixed / total).astype(jnp.bfloat16)
        pltpu.make_async_remote_copy(
            src_ref=abuf.at[h], dst_ref=rbuf.at[h], send_sem=a_send.at[h], recv_sem=a_recv.at[h],
            device_id=after, device_id_type=MESH,
        ).start()

    def finish(h):
        pltpu.make_async_copy(rbuf.at[h], rbuf.at[h], a_recv.at[h]).wait()
        attn = rbuf[h].astype(jnp.float32)
        out_ref[:, cols(h)] = (attn * gate[pl.ds(h, 1), :]).astype(jnp.bfloat16)
        cot = cotv[:, cols(h)].astype(jnp.float32)
        cbuf[0, pl.ds(h, 1), :] = jnp.sum(attn * cot, axis=0, keepdims=True)

    @pl.loop(0, heads)
    def _(h):
        attend(h)

        @pl.when(h >= LAG)
        def _():
            finish(h - LAG)

    @pl.loop(max(heads - LAG, 0), heads)
    def _(h):
        finish(h)

    for r in range(1, n):
        pltpu.make_async_remote_copy(
            src_ref=cbuf.at[0], dst_ref=cbuf.at[r], send_sem=c_send, recv_sem=c_recv,
            device_id=peers[r - 1], device_id_type=MESH,
        ).start()
    pltpu.make_async_copy(cbuf.at[pl.ds(1, n - 1)], cbuf.at[pl.ds(1, n - 1)], c_recv).wait()

    @pl.loop(0, heads)
    def _(h):
        acc = ebuf[0] * cbuf[0, pl.ds(h, 1), :]
        for j in range(1, n):
            acc = acc + ebuf[j] * cbuf[j, pl.ds(h, 1), :]
        grad_ref[:, cols(h)] = acc

    gain_copy.wait_send()
    pltpu.make_async_copy(tbuf.at[pl.ds(1, n - 1)], tbuf.at[pl.ds(1, n - 1)], t_send).wait()
    pltpu.make_async_copy(cbuf.at[pl.ds(1, n - 1)], cbuf.at[pl.ds(1, n - 1)], c_send).wait()

    @pl.loop(0, heads)
    def _(h):
        sent = kv.at[h, :, pl.ds(count, (C - 1) * count), :]
        pltpu.make_async_copy(sent, sent, kv_send.at[h]).wait()
        pltpu.make_async_copy(abuf.at[h], abuf.at[h], a_send.at[h]).wait()


def local(S, C, D, qkv, qk_gain, mod_weight, positions, timesteps, cotangent):
    count, _, width = qkv.shape[2:]
    freqs = mod_weight.shape[1]
    heads = width // HEAD_DIM
    n = C * D
    rows = freqs // n
    hd = HEAD_DIM
    padded = -(-heads // 8) * 8
    bf, f32 = jnp.bfloat16, jnp.float32
    vmem = pl.BlockSpec(memory_space=pltpu.VMEM)
    hbm = pl.BlockSpec(memory_space=pl.ANY)
    dma = pltpu.SemaphoreType.DMA
    attn_out, grad = pl.pallas_call(
        functools.partial(body, S, C, D, heads, freqs),
        out_shape=(
            jax.ShapeDtypeStruct((count, width), bf),
            jax.ShapeDtypeStruct((rows, width), f32),
        ),
        in_specs=[hbm, vmem, hbm, vmem, pl.BlockSpec(memory_space=pltpu.SMEM), hbm, vmem],
        out_specs=(vmem, vmem),
        scratch_shapes=[
            pltpu.VMEM((3, count, width), bf),
            pltpu.VMEM((freqs, width), f32),
            pltpu.VMEM((count, width), bf),
            pltpu.VMEM((heads, 2, C * count, hd), bf),
            pltpu.VMEM((heads, count, hd), bf),
            pltpu.VMEM((heads, count, hd), bf),
            pltpu.VMEM((heads, count, hd), bf),
            pltpu.VMEM((2, width), f32),
            pltpu.VMEM((n, 8, hd), f32),
            pltpu.VMEM((n, rows, hd), f32),
            pltpu.VMEM((n, padded, hd), f32),
            pltpu.VMEM((padded, hd), f32),
            pltpu.VMEM((count, hd), f32),
            pltpu.VMEM((count, hd), f32),
            dma((5,)),
            dma((heads,)), dma((heads,)), dma((heads,)), dma((heads,)),
            dma, dma, dma, dma, dma, dma,
        ],
        compiler_params=pltpu.CompilerParams(
            collective_id=0, has_side_effects=True, vmem_limit_bytes=60 << 20
        ),
    )(
        jnp.moveaxis(qkv[0, 0], 1, 0),
        qk_gain[0],
        mod_weight[0],
        positions.reshape(count, 1),
        timesteps,
        cotangent[0, 0],
        jnp.asarray(rope_freqs()),
    )
    return attn_out[None, None], grad[None]


def solution(mesh):
    sizes = mesh.shape
    return jax.shard_map(
        functools.partial(local, sizes["segment"], sizes["ctx"], sizes["dp"]),
        mesh=mesh,
        in_specs=(
            P("segment", "dp", "ctx", None, None),
            P("segment", None, None),
            P("segment", None, None),
            P("dp", "ctx"),
            P("segment", "dp"),
            P("segment", "dp", "ctx", None),
        ),
        out_specs=(P("segment", "dp", "ctx", None), P("segment", ("ctx", "dp"), None)),
        check_vma=False,
    )
```

time: 162 us -> 60.4 us (0.37)
  waiting for transfers between devices: 97.2 us -> 0 us
  Pallas kernels: 0 us -> 53.6 us
  other arithmetic: 21 us -> 0 us
  between operations: 14.6 us -> 1.29 us
  matrix products: 10.3 us -> 0 us
  starting transfers between devices: 6.79 us -> 0 us
  local copies, waits for them, and re-layouts: 11.9 us -> 5.23 us
    pallas_call x0 -> x1, Pallas kernels: none -> 53.6 us  [local(): pl.pallas_call(functools.partial(body, S, C, D, heads, freqs), out_shape=...]
    reduce_scatter x1 -> x0, waiting for transfers between devices: 41.9 us -> none  [local(): lax.psum_scatter(term, ('ctx', 'dp'), scatter_dimension=0, tiled=True)]
    all_gather x2 -> x0, waiting for transfers between devices: 37.2 us -> none  [the longest x1 23.1 us: section_attention(): lax.all_gather(values, 'ctx', axis=1, tiled=True)]
    ppermute x2 -> x0, waiting for transfers between devices: 18.1 us -> none  [shifted(): lax.ppermute(value, axis, [(i, (i + by) % length) for i in range(length)])]
    dot_general x3 -> x0, matrix products: 10.3 us -> none  [the longest x1 4.7 us: attend(): jnp.einsum('hqd,hkd->hqk', queries, key_block, preferred_element_type=jnp...]
    ppermute x2 -> x0, starting transfers between devices: 6.67 us -> none  [shifted(): lax.ppermute(value, axis, [(i, (i + by) % length) for i in range(length)])]
    mul x3 -> x0, other arithmetic: 5.83 us -> none  [the longest x2 4.08 us: normalize(): return values * lax.rsqrt(mean_sq + 1e-06) * gain]
    convert_element_type x3 -> x0, local copies, waits for them, and re-layouts: 5.47 us -> none  [the longest x1 2.72 us: section_attention(): block[:, 0].astype(jnp.float32)]
  transfers between devices with their start and end apart: 5 -> 0, of which waited for: 4 -> 0; matrix products, arithmetic and copies ran while one was open for 18% -> 0% of each run, Pallas kernels for 0% -> 0%
where the time goes in v1:
time: 60.4 us; the launch traced here: 60.1 us
  Pallas kernels  53.6 us (89%)
  local copies, waits for them, and re-layouts  5.23 us (9%)
  between operations  1.29 us (2%)
    pallas_call x1, Pallas kernels, local(): pl.pallas_call(functools.partial(body, S, C, D, heads, freqs), out_shape=...  53.6 us
    unnamed x2, local copies, waits for them, and re-layouts  3.81 us
    reshape x1, local copies, waits for them, and re-layouts, local(): positions.reshape(count, 1)  1.43 us

profile of v1, /device:TPU:0, one launch (start us, length us, event | category | flops | bytes accessed | tf_op | source)
XLA Modules:
  0.0 60.1 jit_solution(10449200958868414085)
XLA Ops:
  1.3 1.4 %copy.9.pos_ref = s32[160,1]{1,0:T(8,128)} copy(s32[160,1]{0,1:T(1,128)} %bitcast.15) | data formatting | bytes 1280 | tf_op jit(solution)/shard_map/reshape | solution.py:305
  2.7 53.6 %shard_map.86 = (bf16[160,2560]{1,0:T(8,128)(2,1)}, f32[32,2560]{1,0:T(8,128)}) custom-call(bf16[3,160,2560]{2,1,0:T(8,128)(2,1)} %bitcast.10, f32[2,2560]{1,0:T(2,128)} %bitcast.14, f32[256,2560]{1,0:T(8,128)} %bitcast.9, s32[160,1]{1,0:T(8,128)} %copy.9.pos_ref, s32[1,1]{1,0:T(1,128)S(6)} %copy.12.t_ref, bf16[160,2560]{1,0:T(8,128)(2,1)} %bitcast.11, ...), custom_call_target="tpu_custom_call" | custom-call | tf_op jit(solution)/shard_map/pallas_call | solution.py:271
  56.3 2.1 %copy.13 = bf16[1,1,160,2560]{3,2,1,0:T(8,128)(2,1)} copy(bf16[1,1,160,2560]{3,2,1,0:T(8,128)(2,1)} %bitcast.12) | data formatting | bytes 1638400
  58.4 1.7 %copy.14 = f32[1,32,2560]{2,1,0:T(8,128)} copy(f32[1,32,2560]{2,1,0:T(8,128)} %bitcast.13) | data formatting | bytes 655360

commit v2 on v1

--- a/solution.py
+++ b/solution.py
@@ -3,7 +3,6 @@
 
 import jax
 import jax.numpy as jnp
-import numpy as np
 from jax import lax
 from jax.experimental import pallas as pl
 from jax.experimental.pallas import tpu as pltpu
@@ -15,6 +14,7 @@
 MESH = pl.DeviceIdType.MESH
 LEAD = 8
 LAG = 4
+VMEM_LIMIT = 24 << 20
 
 
 def sincos(angle):
@@ -36,23 +36,26 @@
     return s, c
 
 
-def rope_freqs():
-    half = HEAD_DIM // 2
-    side = HEAD_DIM // 6
+def rope_angles(pos):
+    count, hd = pos.shape
+    half = hd // 2
+    side = hd // 6
     first = half - 2 * side
-    rows = np.zeros((8, HEAD_DIM), np.float64)
-    start = 0
-    for group, count in enumerate((first, side, side)):
-        for j in range(count):
-            for lane in (start + j, start + j + half):
-                rows[group, lane] = 10000.0 ** (-j / count)
-        start += count
-    return rows.astype(np.float32)
+    pair = lax.broadcasted_iota(jnp.int32, (8, hd), 1) % half
+    group = jnp.where(pair < first, 0, jnp.where(pair < first + side, 1, 2))
+    offset = jnp.where(group == 0, 0, jnp.where(group == 1, first, first + side))
+    pairs_in = jnp.where(group == 0, first, side).astype(jnp.float32)
+    freq = jnp.exp((pair - offset).astype(jnp.float32) / pairs_in * -math.log(10000.0))[0:1]
+    group = group[0:1]
+    frame = (pos // (GRID_ROWS * GRID_COLS)).astype(jnp.float32)
+    row = (pos // GRID_COLS % GRID_ROWS).astype(jnp.float32)
+    col = (pos % GRID_COLS).astype(jnp.float32)
+    return jnp.where(group == 0, frame, jnp.where(group == 1, row, col)) * freq
 
 
 def body(
     S, C, D, heads, freqs,
-    x_ref, gain_ref, w_ref, pos_ref, t_ref, cot_ref, freq_ref,
+    x_ref, gain_ref, w_ref, pos_ref, t_ref, cot_ref,
     out_ref, grad_ref,
     xv, wv, cotv, kv, qbuf, abuf, rbuf, gains, tbuf, ebuf, cbuf, gate, cosv, sinv,
     load_sem, kv_send, kv_recv, a_send, a_recv, g_send, g_recv, t_send, t_recv, c_send, c_recv,
@@ -129,12 +132,8 @@
             device_id=peers[r - 1], device_id_type=MESH,
         ).start()
 
-    pos = jnp.broadcast_to(pos_ref[...], (count, hd))
-    frame = (pos // (GRID_ROWS * GRID_COLS)).astype(jnp.float32)
-    row = (pos // GRID_COLS % GRID_ROWS).astype(jnp.float32)
-    col = (pos % GRID_COLS).astype(jnp.float32)
-    angle = frame * freq_ref[0:1, :] + row * freq_ref[1:2, :] + col * freq_ref[2:3, :]
-    s, c = sincos(angle)
+    pos = jnp.transpose(jnp.broadcast_to(pos_ref[...], (hd, count)))
+    s, c = sincos(rope_angles(pos))
     lane = lax.broadcasted_iota(jnp.int32, (count, hd), 1)
     cosv[...] = c
     sinv[...] = jnp.where(lane < hd // 2, -s, s)
@@ -266,15 +265,16 @@
     padded = -(-heads // 8) * 8
     bf, f32 = jnp.bfloat16, jnp.float32
     vmem = pl.BlockSpec(memory_space=pltpu.VMEM)
-    hbm = pl.BlockSpec(memory_space=pl.ANY)
+    hbm = pl.BlockSpec(memory_space=pltpu.HBM)
     dma = pltpu.SemaphoreType.DMA
+    pin = functools.partial(pltpu.with_memory_space_constraint, memory_space=pltpu.HBM)
     attn_out, grad = pl.pallas_call(
         functools.partial(body, S, C, D, heads, freqs),
         out_shape=(
             jax.ShapeDtypeStruct((count, width), bf),
             jax.ShapeDtypeStruct((rows, width), f32),
         ),
-        in_specs=[hbm, vmem, hbm, vmem, pl.BlockSpec(memory_space=pltpu.SMEM), hbm, vmem],
+        in_specs=[hbm, hbm, hbm, vmem, pl.BlockSpec(memory_space=pltpu.SMEM), hbm],
         out_specs=(vmem, vmem),
         scratch_shapes=[
             pltpu.VMEM((3, count, width), bf),
@@ -296,16 +296,15 @@
             dma, dma, dma, dma, dma, dma,
         ],
         compiler_params=pltpu.CompilerParams(
-            collective_id=0, has_side_effects=True, vmem_limit_bytes=60 << 20
+            collective_id=0, has_side_effects=True, vmem_limit_bytes=VMEM_LIMIT if C <= 2 else 60 << 20
         ),
     )(
-        jnp.moveaxis(qkv[0, 0], 1, 0),
-        qk_gain[0],
-        mod_weight[0],
-        positions.reshape(count, 1),
+        pin(jnp.moveaxis(qkv[0, 0], 1, 0)),
+        pin(qk_gain[0]),
+        pin(mod_weight[0]),
+        pin(positions),
         timesteps,
-        cotangent[0, 0],
-        jnp.asarray(rope_freqs()),
+        pin(cotangent[0, 0]),
     )
     return attn_out[None, None], grad[None]
 

time: 60.4 us -> 55.5 us (0.919)
  local copies, waits for them, and re-layouts: 5.23 us -> 1.62 us
  Pallas kernels: 53.6 us -> 52.4 us
    unnamed x2, local copies, waits for them, and re-layouts: 3.81 us -> 1.62 us
    reshape x1 -> x0, local copies, waits for them, and re-layouts: 1.43 us -> none  [local(): positions.reshape(count, 1)]
    pallas_call x1, Pallas kernels: 53.6 us -> 52.4 us  [local(): pl.pallas_call(functools.partial(body, S, C, D, heads, freqs), out_shape=...]
where the time goes in v2:
time: 55.5 us; the launch traced here: 55.3 us
  Pallas kernels  52.4 us (94%)
  local copies, waits for them, and re-layouts  1.62 us (3%)
  between operations  1.29 us (2%)
    pallas_call x1, Pallas kernels, local(): pl.pallas_call(functools.partial(body, S, C, D, heads, freqs), out_shape=...  52.4 us
    unnamed x2, local copies, waits for them, and re-layouts  1.62 us

profile of v2, /device:TPU:0, one launch (start us, length us, event | category | flops | bytes accessed | tf_op | source)
XLA Modules:
  0.0 55.3 jit_solution(10511737070469885769)
XLA Ops:
  1.3 52.4 %shard_map.77 = (bf16[160,2560]{1,0:T(8,128)(2,1)S(1)}, f32[32,2560]{1,0:T(8,128)S(1)}) custom-call(bf16[3,160,2560]{2,1,0:T(8,128)(2,1)} %bitcast.11, f32[2,2560]{1,0:T(2,128)} %bitcast.13, f32[256,2560]{1,0:T(8,128)} %bitcast.10, s32[1,160]{1,0:T(1,128)} %pos_ref.1, s32[1,1]{1,0:T(1,128)S(6)} %copy.10.t_ref, bf16[160,2560]{1,0:T(8,128)(2,1)} %bitcast.12), custom_call_target="tpu_custom_call" | custom-call | tf_op jit(solution)/shard_map/pallas_call | solution.py:271
  53.7 0.9 %copy.11 = bf16[1,1,160,2560]{3,2,1,0:T(8,128)(2,1)} copy(bf16[1,1,160,2560]{3,2,1,0:T(8,128)(2,1)S(1)} %bitcast.8) | data formatting | bytes 1638400
  54.6 0.7 %copy.12 = f32[1,32,2560]{2,1,0:T(8,128)} copy(f32[1,32,2560]{2,1,0:T(8,128)S(1)} %bitcast.9) | data formatting | bytes 655360

commit v3 on v2

--- a/solution.py
+++ b/solution.py
@@ -14,6 +14,8 @@
 MESH = pl.DeviceIdType.MESH
 LEAD = 8
 LAG = 4
+DIRECT = 4
+FORWARD_AT = 6
 VMEM_LIMIT = 24 << 20
 
 
@@ -57,13 +59,15 @@
     S, C, D, heads, freqs,
     x_ref, gain_ref, w_ref, pos_ref, t_ref, cot_ref,
     out_ref, grad_ref,
-    xv, wv, cotv, kv, qbuf, abuf, rbuf, gains, tbuf, ebuf, cbuf, gate, cosv, sinv,
+    xv, wv, cotv, kv, qbuf, abuf, rbuf, direct, gains, tbuf, ebuf, cbuf, gate, cosv, sinv,
     load_sem, kv_send, kv_recv, a_send, a_recv, g_send, g_recv, t_send, t_recv, c_send, c_recv,
+    b_send, b_recv, bx_send, bx_recv,
 ):
     n = C * D
     count = x_ref.shape[1]
     rows = freqs // n
     hd = HEAD_DIM
+    early = heads - direct.shape[0]
     seg = lax.axis_index("segment")
     ctx = lax.axis_index("ctx")
     dp = lax.axis_index("dp")
@@ -120,7 +124,7 @@
                 device_id=ring[r - 1], device_id_type=MESH,
             ).start()
 
-    lead = min(LEAD, heads)
+    lead = min(LEAD, early)
 
     @pl.loop(0, lead)
     def _(h):
@@ -154,22 +158,47 @@
 
     loads[0].wait()
     inv_k = inverse_norm(1)
+    loads[1].wait()
+    inv_q = inverse_norm(0)
     gain_copy.wait_recv()
 
-    @pl.loop(0, heads)
+    def hand_over(source, part, b):
+        pltpu.make_async_remote_copy(
+            src_ref=source, dst_ref=direct.at[b, part, pl.ds(0, count), :],
+            send_sem=b_send.at[b], recv_sem=b_recv.at[b], device_id=after, device_id_type=MESH,
+        ).start()
+
+    def forward(b):
+        here = direct.at[b, :, pl.ds(0, count), :]
+        pltpu.make_async_copy(here, here, b_recv.at[b]).wait()
+        for r in range(1, C):
+            pltpu.make_async_remote_copy(
+                src_ref=direct.at[b, pl.ds(0, 2), pl.ds(0, count), :],
+                dst_ref=direct.at[b, pl.ds(0, 2), pl.ds(r * count, count), :],
+                send_sem=bx_send.at[b], recv_sem=bx_recv.at[b],
+                device_id=ring[r - 1], device_id_type=MESH,
+            ).start()
+
+    @pl.loop(early, heads)
+    def _(h):
+        kv[h, 0, 0:count, :] = turned(1, h, inv_k)
+        qbuf[h] = turned(0, h, inv_q)
+        hand_over(x_ref.at[2, :, cols(h)], 1, h - early)
+        hand_over(kv.at[h, 0, pl.ds(0, count), :], 0, h - early)
+        hand_over(qbuf.at[h], 2, h - early)
+
+    @pl.loop(0, early)
     def _(h):
         kv[h, 0, 0:count, :] = turned(1, h, inv_k)
         send_keys(h)
 
-        @pl.when(h + lead < heads)
+        @pl.when(h + lead < early)
         def _():
             send_values(h + lead)
 
-    loads[1].wait()
-    inv_q = inverse_norm(0)
     loads[2].wait()
 
-    @pl.loop(0, heads)
+    @pl.loop(0, early)
     def _(h):
         qbuf[h] = turned(0, h, inv_q)
         kv[h, 1, 0:count, :] = xv[2, :, cols(h)]
@@ -196,39 +225,57 @@
 
     scale = 1.0 / hd**0.5
 
+    def mix(queries, keys, values):
+        scores = lax.dot_general(
+            queries, keys, (((1,), (1,)), ((), ())), preferred_element_type=jnp.float32
+        ) * scale
+        expo = jnp.exp(scores - jnp.max(scores, axis=1, keepdims=True))
+        total = jnp.sum(expo, axis=1, keepdims=True)
+        mixed = jnp.dot(expo.astype(jnp.bfloat16), values, preferred_element_type=jnp.float32)
+        return mixed / total
+
     def attend(h):
         arrived = kv.at[h, :, pl.ds(count, (C - 1) * count), :]
         pltpu.make_async_copy(arrived, arrived, kv_recv.at[h]).wait()
-        scores = lax.dot_general(
-            qbuf[h], kv[h, 0], (((1,), (1,)), ((), ())), preferred_element_type=jnp.float32
-        ) * scale
-        expo = jnp.exp(scores - jnp.max(scores, axis=1, keepdims=True))
-        total = jnp.sum(expo, axis=1, keepdims=True)
-        mixed = jnp.dot(expo.astype(jnp.bfloat16), kv[h, 1], preferred_element_type=jnp.float32)
-        abuf[h] = (mixed / total).astype(jnp.bfloat16)
+        abuf[h] = mix(qbuf[h], kv[h, 0], kv[h, 1]).astype(jnp.bfloat16)
         pltpu.make_async_remote_copy(
             src_ref=abuf.at[h], dst_ref=rbuf.at[h], send_sem=a_send.at[h], recv_sem=a_recv.at[h],
             device_id=after, device_id_type=MESH,
         ).start()
 
-    def finish(h):
-        pltpu.make_async_copy(rbuf.at[h], rbuf.at[h], a_recv.at[h]).wait()
-        attn = rbuf[h].astype(jnp.float32)
+    def use(h, attn):
         out_ref[:, cols(h)] = (attn * gate[pl.ds(h, 1), :]).astype(jnp.bfloat16)
         cot = cotv[:, cols(h)].astype(jnp.float32)
         cbuf[0, pl.ds(h, 1), :] = jnp.sum(attn * cot, axis=0, keepdims=True)
 
-    @pl.loop(0, heads)
+    def finish(h):
+        pltpu.make_async_copy(rbuf.at[h], rbuf.at[h], a_recv.at[h]).wait()
+        use(h, rbuf[h].astype(jnp.float32))
+
+    @pl.loop(0, early)
     def _(h):
         attend(h)
+
+        @pl.when(h == min(FORWARD_AT, early - 1))
+        def _():
+            @pl.loop(0, heads - early)
+            def _(b):
+                forward(b)
 
         @pl.when(h >= LAG)
         def _():
             finish(h - LAG)
 
-    @pl.loop(max(heads - LAG, 0), heads)
+    @pl.loop(max(early - LAG, 0), early)
     def _(h):
         finish(h)
+
+    @pl.loop(early, heads)
+    def _(h):
+        b = h - early
+        arrived = direct.at[b, pl.ds(0, 2), pl.ds(count, (C - 1) * count), :]
+        pltpu.make_async_copy(arrived, arrived, bx_recv.at[b]).wait()
+        use(h, mix(direct[b, 2, 0:count, :], direct[b, 0], direct[b, 1]))
 
     for r in range(1, n):
         pltpu.make_async_remote_copy(
@@ -248,7 +295,14 @@
     pltpu.make_async_copy(tbuf.at[pl.ds(1, n - 1)], tbuf.at[pl.ds(1, n - 1)], t_send).wait()
     pltpu.make_async_copy(cbuf.at[pl.ds(1, n - 1)], cbuf.at[pl.ds(1, n - 1)], c_send).wait()
 
-    @pl.loop(0, heads)
+    @pl.loop(0, heads - early)
+    def _(b):
+        handed = direct.at[b, :, pl.ds(0, count), :]
+        pltpu.make_async_copy(handed, handed, b_send.at[b]).wait()
+        sent = direct.at[b, pl.ds(0, 2), pl.ds(count, (C - 1) * count), :]
+        pltpu.make_async_copy(sent, sent, bx_send.at[b]).wait()
+
+    @pl.loop(0, early)
     def _(h):
         sent = kv.at[h, :, pl.ds(count, (C - 1) * count), :]
         pltpu.make_async_copy(sent, sent, kv_send.at[h]).wait()
@@ -262,6 +316,7 @@
     n = C * D
     rows = freqs // n
     hd = HEAD_DIM
+    last = min(DIRECT, heads - 1)
     padded = -(-heads // 8) * 8
     bf, f32 = jnp.bfloat16, jnp.float32
     vmem = pl.BlockSpec(memory_space=pltpu.VMEM)
@@ -284,6 +339,7 @@
             pltpu.VMEM((heads, count, hd), bf),
             pltpu.VMEM((heads, count, hd), bf),
             pltpu.VMEM((heads, count, hd), bf),
+            pltpu.VMEM((last, 3, C * count, hd), bf),
             pltpu.VMEM((2, width), f32),
             pltpu.VMEM((n, 8, hd), f32),
             pltpu.VMEM((n, rows, hd), f32),
@@ -294,6 +350,7 @@
             dma((5,)),
             dma((heads,)), dma((heads,)), dma((heads,)), dma((heads,)),
             dma, dma, dma, dma, dma, dma,
+            dma((last,)), dma((last,)), dma((last,)), dma((last,)),
         ],
         compiler_params=pltpu.CompilerParams(
             collective_id=0, has_side_effects=True, vmem_limit_bytes=VMEM_LIMIT if C <= 2 else 60 << 20

time: 55.5 us -> 51.7 us (0.932)
  Pallas kernels: 52.4 us -> 48.6 us
    pallas_call x1, Pallas kernels: 52.4 us -> 48.6 us  [local(): pl.pallas_call(functools.partial(body, S, C, D, heads, freqs), out_shape=...]
where the time goes in v3:
time: 51.7 us; the launch traced here: 51.5 us
  Pallas kernels  48.6 us (94%)
  local copies, waits for them, and re-layouts  1.62 us (3%)
  between operations  1.29 us (2%)
    pallas_call x1, Pallas kernels, local(): pl.pallas_call(functools.partial(body, S, C, D, heads, freqs), out_shape=...  48.6 us
    unnamed x2, local copies, waits for them, and re-layouts  1.62 us

profile of v3, /device:TPU:0, one launch (start us, length us, event | category | flops | bytes accessed | tf_op | source)
XLA Modules:
  0.0 51.5 jit_solution(3538593385409010422)
XLA Ops:
  1.3 48.6 %shard_map.77 = (bf16[160,2560]{1,0:T(8,128)(2,1)S(1)}, f32[32,2560]{1,0:T(8,128)S(1)}) custom-call(bf16[3,160,2560]{2,1,0:T(8,128)(2,1)} %bitcast.11, f32[2,2560]{1,0:T(2,128)} %bitcast.13, f32[256,2560]{1,0:T(8,128)} %bitcast.10, s32[1,160]{1,0:T(1,128)} %pos_ref.1, s32[1,1]{1,0:T(1,128)S(6)} %copy.10.t_ref, bf16[160,2560]{1,0:T(8,128)(2,1)} %bitcast.12), custom_call_target="tpu_custom_call" | custom-call | tf_op jit(solution)/shard_map/pallas_call | solution.py:326
  49.9 0.9 %copy.11 = bf16[1,1,160,2560]{3,2,1,0:T(8,128)(2,1)} copy(bf16[1,1,160,2560]{3,2,1,0:T(8,128)(2,1)S(1)} %bitcast.8) | data formatting | bytes 1638400
  50.8 0.7 %copy.12 = f32[1,32,2560]{2,1,0:T(8,128)} copy(f32[1,32,2560]{2,1,0:T(8,128)S(1)} %bitcast.9) | data formatting | bytes 655360

commit v4 on v3

--- a/solution.py
+++ b/solution.py
@@ -58,10 +58,10 @@
 def body(
     S, C, D, heads, freqs,
     x_ref, gain_ref, w_ref, pos_ref, t_ref, cot_ref,
-    out_ref, grad_ref,
-    xv, wv, cotv, kv, qbuf, abuf, rbuf, direct, gains, tbuf, ebuf, cbuf, gate, cosv, sinv,
+    out_ref, cbuf, ebuf,
+    xv, wv, cotv, kv, qbuf, abuf, rbuf, direct, gains, tbuf, gate, cosv, sinv,
     load_sem, kv_send, kv_recv, a_send, a_recv, g_send, g_recv, t_send, t_recv, c_send, c_recv,
-    b_send, b_recv, bx_send, bx_recv,
+    b_send, b_recv, bx_send, bx_recv, down_sem, up_sem,
 ):
     n = C * D
     count = x_ref.shape[1]
@@ -96,15 +96,32 @@
     tbuf[0] = jnp.full((8, hd), step, jnp.float32)
 
     barrier = pltpu.get_barrier_semaphore()
-    for who in peers + [after, before]:
+    def greet(who):
         pl.semaphore_signal(barrier, inc=1, device_id=who, device_id_type=MESH)
-    pl.semaphore_wait(barrier, n + 1)
+
+    for who in peers:
+        greet(who)
+    chain = S > 2
+    if chain:
+        @pl.when(seg < S - 1)
+        def _():
+            greet(after)
+
+        @pl.when(seg > 0)
+        def _():
+            greet(before)
+
+        ends = jnp.where(seg == 0, 1, 0) + jnp.where(seg == S - 1, 1, 0)
+        pl.semaphore_wait(barrier, n + 1 - ends)
+    else:
+        greet(after)
+        greet(before)
+        pl.semaphore_wait(barrier, n + 1)
 
     gain_copy = pltpu.make_async_remote_copy(
         src_ref=gain_ref, dst_ref=gains, send_sem=g_send, recv_sem=g_recv,
         device_id=before, device_id_type=MESH,
     )
-    gain_copy.start()
 
     def send_values(h):
         for r in range(1, C):
@@ -135,6 +152,44 @@
             src_ref=tbuf.at[0], dst_ref=tbuf.at[r], send_sem=t_send, recv_sem=t_recv,
             device_id=peers[r - 1], device_id_type=MESH,
         ).start()
+
+    def tell(sem, who):
+        pl.semaphore_signal(sem, inc=1, device_id=who, device_id_type=MESH)
+
+    if chain:
+        @pl.when(seg > 0)
+        def _():
+            gain_copy.start()
+
+        @pl.when(seg == S - 2)
+        def _():
+            tell(down_sem, before)
+
+        @pl.when(seg == 1)
+        def _():
+            tell(up_sem, after)
+
+        @pl.when(seg < S - 2)
+        def _():
+            pl.semaphore_wait(down_sem, 1)
+
+            @pl.when(seg > 0)
+            def _():
+                tell(down_sem, before)
+
+        @pl.when(seg == 0)
+        def _():
+            gain_copy.start()
+
+        @pl.when(seg > 1)
+        def _():
+            pl.semaphore_wait(up_sem, 1)
+
+            @pl.when(seg < S - 1)
+            def _():
+                tell(up_sem, after)
+    else:
+        gain_copy.start()
 
     pos = jnp.transpose(jnp.broadcast_to(pos_ref[...], (hd, count)))
     s, c = sincos(rope_angles(pos))
@@ -284,13 +339,6 @@
         ).start()
     pltpu.make_async_copy(cbuf.at[pl.ds(1, n - 1)], cbuf.at[pl.ds(1, n - 1)], c_recv).wait()
 
-    @pl.loop(0, heads)
-    def _(h):
-        acc = ebuf[0] * cbuf[0, pl.ds(h, 1), :]
-        for j in range(1, n):
-            acc = acc + ebuf[j] * cbuf[j, pl.ds(h, 1), :]
-        grad_ref[:, cols(h)] = acc
-
     gain_copy.wait_send()
     pltpu.make_async_copy(tbuf.at[pl.ds(1, n - 1)], tbuf.at[pl.ds(1, n - 1)], t_send).wait()
     pltpu.make_async_copy(cbuf.at[pl.ds(1, n - 1)], cbuf.at[pl.ds(1, n - 1)], c_send).wait()
@@ -307,6 +355,21 @@
         sent = kv.at[h, :, pl.ds(count, (C - 1) * count), :]
         pltpu.make_async_copy(sent, sent, kv_send.at[h]).wait()
         pltpu.make_async_copy(abuf.at[h], abuf.at[h], a_send.at[h]).wait()
+
+
+def store(n, heads, attn_ref, chan_ref, emb_ref, out_ref, grad_ref, total, out_sem, grad_sem):
+    copy = pltpu.make_async_copy(attn_ref, out_ref, out_sem)
+    copy.start()
+    hd = HEAD_DIM
+    for h in range(heads):
+        acc = emb_ref[0] * chan_ref[0, h : h + 1, :]
+        for j in range(1, n):
+            acc = acc + emb_ref[j] * chan_ref[j, h : h + 1, :]
+        total[h] = acc
+        pltpu.make_async_copy(total.at[h], grad_ref.at[:, h * hd : (h + 1) * hd], grad_sem.at[h]).start()
+    for h in range(heads):
+        pltpu.make_async_copy(total.at[h], grad_ref.at[:, h * hd : (h + 1) * hd], grad_sem.at[h]).wait()
+    copy.wait()
 
 
 def local(S, C, D, qkv, qk_gain, mod_weight, positions, timesteps, cotangent):
@@ -323,14 +386,15 @@
     hbm = pl.BlockSpec(memory_space=pltpu.HBM)
     dma = pltpu.SemaphoreType.DMA
     pin = functools.partial(pltpu.with_memory_space_constraint, memory_space=pltpu.HBM)
-    attn_out, grad = pl.pallas_call(
+    attn, chans, embs = pl.pallas_call(
         functools.partial(body, S, C, D, heads, freqs),
         out_shape=(
             jax.ShapeDtypeStruct((count, width), bf),
-            jax.ShapeDtypeStruct((rows, width), f32),
+            jax.ShapeDtypeStruct((n, padded, hd), f32),
+            jax.ShapeDtypeStruct((n, rows, hd), f32),
         ),
         in_specs=[hbm, hbm, hbm, vmem, pl.BlockSpec(memory_space=pltpu.SMEM), hbm],
-        out_specs=(vmem, vmem),
+        out_specs=(vmem, vmem, vmem),
         scratch_shapes=[
             pltpu.VMEM((3, count, width), bf),
             pltpu.VMEM((freqs, width), f32),
@@ -342,8 +406,6 @@
             pltpu.VMEM((last, 3, C * count, hd), bf),
             pltpu.VMEM((2, width), f32),
             pltpu.VMEM((n, 8, hd), f32),
-            pltpu.VMEM((n, rows, hd), f32),
-            pltpu.VMEM((n, padded, hd), f32),
             pltpu.VMEM((padded, hd), f32),
             pltpu.VMEM((count, hd), f32),
             pltpu.VMEM((count, hd), f32),
@@ -351,6 +413,7 @@
             dma((heads,)), dma((heads,)), dma((heads,)), dma((heads,)),
             dma, dma, dma, dma, dma, dma,
             dma((last,)), dma((last,)), dma((last,)), dma((last,)),
+            pltpu.SemaphoreType.REGULAR, pltpu.SemaphoreType.REGULAR,
         ],
         compiler_params=pltpu.CompilerParams(
             collective_id=0, has_side_effects=True, vmem_limit_bytes=VMEM_LIMIT if C <= 2 else 60 << 20
@@ -363,6 +426,17 @@
         timesteps,
         pin(cotangent[0, 0]),
     )
+    attn_out, grad = pl.pallas_call(
+        functools.partial(store, n, heads),
+        out_shape=(
+            jax.ShapeDtypeStruct((count, width), bf),
+            jax.ShapeDtypeStruct((rows, width), f32),
+        ),
+        in_specs=[pl.BlockSpec(memory_space=pl.ANY), vmem, vmem],
+        out_specs=(pl.BlockSpec(memory_space=pl.ANY), pl.BlockSpec(memory_space=pl.ANY)),
+        scratch_shapes=[pltpu.VMEM((heads, rows, hd), f32), dma, dma((heads,))],
+        compiler_params=pltpu.CompilerParams(vmem_limit_bytes=4 << 20),
+    )(attn, chans, embs)
     return attn_out[None, None], grad[None]
 
 

time: 51.7 us -> 50 us (0.967)
  local copies, waits for them, and re-layouts: 1.62 us -> 0 us
    unnamed x2 -> x0, local copies, waits for them, and re-layouts: 1.62 us -> none
    pallas_call x1, Pallas kernels: 48.6 us -> 47.4 us  [local(): pl.pallas_call(functools.partial(body, S, C, D, heads, freqs), out_shape=...]
    pallas_call x0 -> x1, Pallas kernels: none -> 1.17 us  [local(): pl.pallas_call(functools.partial(store, n, heads), out_shape=(jax.ShapeDt...]
where the time goes in v4:
time: 50 us; the launch traced here: 49.8 us
  Pallas kernels  48.6 us (97%)
  between operations  1.29 us (3%)
    pallas_call x1, Pallas kernels, local(): pl.pallas_call(functools.partial(body, S, C, D, heads, freqs), out_shape=...  47.4 us
    pallas_call x1, Pallas kernels, local(): pl.pallas_call(functools.partial(store, n, heads), out_shape=(jax.ShapeDt...  1.17 us

profile of v4, /device:TPU:0, one launch (start us, length us, event | category | flops | bytes accessed | tf_op | source)
XLA Modules:
  0.0 49.8 jit_solution(16699085112034263065)
XLA Ops:
  1.3 47.4 %shard_map.77 = (bf16[160,2560]{1,0:T(8,128)(2,1)S(1)}, f32[8,24,128]{2,1,0:T(8,128)S(1)}, f32[8,32,128]{2,1,0:T(8,128)S(1)}) custom-call(bf16[3,160,2560]{2,1,0:T(8,128)(2,1)} %bitcast.9, f32[2,2560]{1,0:T(2,128)} %bitcast.11, f32[256,2560]{1,0:T(8,128)} %bitcast.8, s32[1,160]{1,0:T(1,128)} %pos_ref.1, s32[1,1]{1,0:T(1,128)S(6)} %copy.8.t_ref, ...), custom_call_target="tpu_custom_call" | custom-call | tf_op jit(solution)/shard_map/pallas_call | solution.py:389
  48.7 1.2 %shard_map.78 = (bf16[160,2560]{1,0:T(8,128)(2,1)}, f32[32,2560]{1,0:T(8,128)}) custom-call(bf16[160,2560]{1,0:T(8,128)(2,1)S(1)} %get-tuple-element.7.attn_ref, f32[8,24,128]{2,1,0:T(8,128)S(1)} %get-tuple-element.8.chan_ref, f32[8,32,128]{2,1,0:T(8,128)S(1)} %get-tuple-element.9.emb_ref), custom_call_target="tpu_custom_call" | custom-call | tf_op jit(solution)/shard_map/pallas_call | solution.py:429

commit v5 on v4

--- a/solution.py
+++ b/solution.py
@@ -13,8 +13,8 @@
 GRID_COLS = 80
 MESH = pl.DeviceIdType.MESH
 LEAD = 8
-LAG = 4
-DIRECT = 4
+LAG = 6
+DIRECT = 5
 FORWARD_AT = 6
 VMEM_LIMIT = 24 << 20
 
@@ -325,6 +325,20 @@
     def _(h):
         finish(h)
 
+    split = early // 8 * 8
+
+    def share_sums(low, high, part):
+        for r in range(1, n):
+            pltpu.make_async_remote_copy(
+                src_ref=cbuf.at[0, pl.ds(low, high - low), :],
+                dst_ref=cbuf.at[r, pl.ds(low, high - low), :],
+                send_sem=c_send.at[part], recv_sem=c_recv.at[part],
+                device_id=peers[r - 1], device_id_type=MESH,
+            ).start()
+
+    if split > 0:
+        share_sums(0, split, 0)
+
     @pl.loop(early, heads)
     def _(h):
         b = h - early
@@ -332,16 +346,19 @@
         pltpu.make_async_copy(arrived, arrived, bx_recv.at[b]).wait()
         use(h, mix(direct[b, 2, 0:count, :], direct[b, 0], direct[b, 1]))
 
-    for r in range(1, n):
-        pltpu.make_async_remote_copy(
-            src_ref=cbuf.at[0], dst_ref=cbuf.at[r], send_sem=c_send, recv_sem=c_recv,
-            device_id=peers[r - 1], device_id_type=MESH,
-        ).start()
-    pltpu.make_async_copy(cbuf.at[pl.ds(1, n - 1)], cbuf.at[pl.ds(1, n - 1)], c_recv).wait()
+    if n > 1:
+        share_sums(split, cbuf.shape[1], 1)
+        for part, (low, high) in enumerate(((0, split), (split, cbuf.shape[1]))):
+            if high > low:
+                others = cbuf.at[pl.ds(1, n - 1), pl.ds(low, high - low), :]
+                pltpu.make_async_copy(others, others, c_recv.at[part]).wait()
 
     gain_copy.wait_send()
     pltpu.make_async_copy(tbuf.at[pl.ds(1, n - 1)], tbuf.at[pl.ds(1, n - 1)], t_send).wait()
-    pltpu.make_async_copy(cbuf.at[pl.ds(1, n - 1)], cbuf.at[pl.ds(1, n - 1)], c_send).wait()
+    for part, (low, high) in enumerate(((0, split), (split, cbuf.shape[1]))):
+        if n > 1 and high > low:
+            others = cbuf.at[pl.ds(1, n - 1), pl.ds(low, high - low), :]
+            pltpu.make_async_copy(others, others, c_send.at[part]).wait()
 
     @pl.loop(0, heads - early)
     def _(b):
@@ -411,7 +428,7 @@
             pltpu.VMEM((count, hd), f32),
             dma((5,)),
             dma((heads,)), dma((heads,)), dma((heads,)), dma((heads,)),
-            dma, dma, dma, dma, dma, dma,
+            dma, dma, dma, dma, dma((2,)), dma((2,)),
             dma((last,)), dma((last,)), dma((last,)), dma((last,)),
             pltpu.SemaphoreType.REGULAR, pltpu.SemaphoreType.REGULAR,
         ],

time: 50 us -> 49.3 us (0.986)
  Pallas kernels: 48.6 us -> 47.9 us
    pallas_call x1, Pallas kernels: 47.4 us -> 46.7 us  [local(): pl.pallas_call(functools.partial(body, S, C, D, heads, freqs), out_shape=...]
where the time goes in v5:
time: 49.3 us; the launch traced here: 49.2 us
  Pallas kernels  47.9 us (97%)
  between operations  1.29 us (3%)
    pallas_call x1, Pallas kernels, local(): pl.pallas_call(functools.partial(body, S, C, D, heads, freqs), out_shape=...  46.7 us
    pallas_call x1, Pallas kernels, local(): pl.pallas_call(functools.partial(store, n, heads), out_shape=(jax.ShapeDt...  1.17 us

profile of v5, /device:TPU:0, one launch (start us, length us, event | category | flops | bytes accessed | tf_op | source)
XLA Modules:
  0.0 49.2 jit_solution(15449150682975746735)
XLA Ops:
  1.3 46.7 %shard_map.77 = (bf16[160,2560]{1,0:T(8,128)(2,1)S(1)}, f32[8,24,128]{2,1,0:T(8,128)S(1)}, f32[8,32,128]{2,1,0:T(8,128)S(1)}) custom-call(bf16[3,160,2560]{2,1,0:T(8,128)(2,1)} %bitcast.9, f32[2,2560]{1,0:T(2,128)} %bitcast.11, f32[256,2560]{1,0:T(8,128)} %bitcast.8, s32[1,160]{1,0:T(1,128)} %pos_ref.1, s32[1,1]{1,0:T(1,128)S(6)} %copy.8.t_ref, ...), custom_call_target="tpu_custom_call" | custom-call | tf_op jit(solution)/shard_map/pallas_call | solution.py:406
  48.0 1.2 %shard_map.78 = (bf16[160,2560]{1,0:T(8,128)(2,1)}, f32[32,2560]{1,0:T(8,128)}) custom-call(bf16[160,2560]{1,0:T(8,128)(2,1)S(1)} %get-tuple-element.7.attn_ref, f32[8,24,128]{2,1,0:T(8,128)S(1)} %get-tuple-element.8.chan_ref, f32[8,32,128]{2,1,0:T(8,128)S(1)} %get-tuple-element.9.emb_ref), custom_call_target="tpu_custom_call" | custom-call | tf_op jit(solution)/shard_map/pallas_call | solution.py:446
